TPU v7x, 32 devices: a whole 2x2x4 slice. The times are simulated.
32 devices in a mesh: head: 4 (over x, core), seq: 8 (over z, y).
Axes of the slice: x: 2, y: 2, z: 4, core: 2. Of those that a mesh axis runs over, the one named last changes fastest.
Arguments:
- skip_stream: bfloat16 [4096, 1024], P('head', 'seq'), may hold values from -6 to 6
- acceptance_vector: bfloat16 [4096, 1024], P('head', 'seq'), may hold values from -6 to 6
- address_vectors: bfloat16 [4096, 1024], P('head', 'seq'), may hold values from -0.75 to 0.75
- content_vectors: bfloat16 [4096, 1024], P('head', 'seq'), may hold values from -6 to 6
- emission_valve: bfloat16 [4096, 1024], P('head', 'seq'), may hold values from -6 to 6
- fading_exponent: bfloat16 [4096, 1024], P('head', 'seq'), may hold values from -0.7 to 0
- adaptation_speed: bfloat16 [4096, 1024], P('head', 'seq'), may hold values from 0 to 0.9
- erasure_factor: float32 [4096], P('head'), may hold values from 0.3 to 3
- reward_coefficient: float32 [4096], P('head'), may hold values from -4 to 4
- cluster_multiplier: float32 [4096], P('head'), may hold values from 0.5 to 2
- cluster_offset: float32 [4096], P('head'), may hold values from -3 to 3
- projection_weights: bfloat16 [4096, 4096], P(None, 'head'), may hold values from -0.125 to 0.125
Outputs:
- layer_output: bfloat16 [4096, 1024], P('head', 'seq')
All inputs are finite; a program needn't handle non-finite values.
Results may differ from a plain program's by a relative error of at most 0.0048.
Values may be sent and summed in bfloat16 or wider, within the bound.
A program may use at most 128 MiB of HBM per device.

v0:
```python
import jax
import jax.numpy as jnp
from jax import lax
from jax.sharding import PartitionSpec as P

UNIT_CHANNELS = 64
SPAN = 64


HIGHEST = lax.Precision.HIGHEST


def from_behind(block, axis, distance):
    devices = range(lax.axis_size(axis))
    route = [(i - distance, i) for i in devices if i - distance in devices]
    return lax.ppermute(block, axis, route)


def contract(form, left, right):
    return jnp.einsum(form, left, right, precision=HIGHEST)


def divided_segments(field, owned_units, owned_segments):
    return jnp.transpose(
        field.astype(jnp.float32).reshape(owned_units, UNIT_CHANNELS, owned_segments, SPAN),
        (0, 2, 1, 3),
    )


def chain_matrices(owned_units):
    identity = jnp.broadcast_to(
        jnp.eye(UNIT_CHANNELS, dtype=jnp.float32), (owned_units, UNIT_CHANNELS, UNIT_CHANNELS)
    )
    return (identity, jnp.zeros((owned_units, UNIT_CHANNELS, UNIT_CHANNELS), jnp.float32))


def incoming_state(transfer, produced):
    identity, empty_state = chain_matrices(transfer.shape[0])

    def relay_once(step_index, arriving):
        return from_behind(contract("hvn,hnk->hvk", arriving, transfer) + produced, "seq", 1)

    return lax.fori_loop(0, lax.axis_size("seq") - 1, relay_once, empty_state)


def on_device(
    skip_stream,
    acceptance_vector,
    address_vectors,
    content_vectors,
    emission_valve,
    fading_exponent,
    adaptation_speed,
    erasure_factor,
    reward_coefficient,
    cluster_multiplier,
    cluster_offset,
    projection_weights,
):
    channels, length = acceptance_vector.shape
    owned_units = channels // UNIT_CHANNELS
    owned_segments = length // SPAN
    acceptance_segment = divided_segments(acceptance_vector, owned_units, owned_segments)
    address_segment = divided_segments(address_vectors, owned_units, owned_segments)
    value_blk = divided_segments(content_vectors, owned_units, owned_segments)
    decay_blk = divided_segments(fading_exponent, owned_units, owned_segments)
    rate_blk = divided_segments(adaptation_speed, owned_units, owned_segments)
    scaled = address_segment * erasure_factor.reshape(owned_units, 1, UNIT_CHANNELS, 1)
    removal = scaled * lax.rsqrt(jnp.sum(scaled * scaled, axis=2, keepdims=True) + 1e-06)
    pulled = rate_blk * removal
    running = jnp.cumsum(decay_blk, axis=3)
    pulled_back = pulled * jnp.exp(-running)
    keys_back = address_segment * jnp.exp(-running)
    removal_fwd = -removal * jnp.exp(running - decay_blk)
    recept_fwd = acceptance_segment * jnp.exp(running)
    to_end = jnp.exp(running[..., -1:] - running)
    block_decay = jnp.exp(running[..., -1])
    positions = jnp.arange(SPAN)
    strictly_before = (positions[:, None] < positions[None, :]).astype(jnp.float32)
    up_to = (positions[:, None] <= positions[None, :]).astype(jnp.float32)
    pair_mix = contract("hcns,hcnt->hcst", pulled_back, removal_fwd) * strictly_before
    key_mix = contract("hcns,hcnt->hcst", keys_back, removal_fwd) * strictly_before
    solved = jnp.concatenate([contract("hcvs,hcst->hcvt", value_blk, key_mix), removal_fwd], axis=2)
    power_mix = pair_mix
    tree_levels = (SPAN - 1).bit_length()
    for level in range(tree_levels):
        solved = solved + contract("hcrs,hcst->hcrt", solved, power_mix)
        if level + 1 < tree_levels:
            power_mix = contract("hcrs,hcst->hcrt", power_mix, power_mix)
    inserted = solved[:, :, :UNIT_CHANNELS]
    through = solved[:, :, UNIT_CHANNELS:]
    pulled_end = pulled * to_end
    block_trans = (
        contract("hcns,hcks->hcnk", through, pulled_end)
        + jnp.eye(UNIT_CHANNELS, dtype=jnp.float32) * block_decay[..., None]
    )
    block_state = contract("hcvs,hcks->hcvk", inserted, pulled_end) + contract(
        "hcvs,hcks->hcvk", value_blk, address_segment * to_end
    )
    trans_seq = jnp.moveaxis(block_trans, 1, 0)
    state_seq = jnp.moveaxis(block_state, 1, 0)
    identity, empty_state = chain_matrices(owned_units)
    pair_read = contract("hcns,hcnt->hcst", pulled_back, recept_fwd) * up_to
    key_read = contract("hcns,hcnt->hcst", keys_back, recept_fwd) * up_to
    local_out = contract("hcvs,hcst->hcvt", inserted, pair_read) + contract(
        "hcvs,hcst->hcvt", value_blk, key_read
    )
    start_read = recept_fwd + contract("hcns,hcst->hcnt", through, pair_read)
    local_out, start_read = (jnp.moveaxis(local_out, 1, 0), jnp.moveaxis(start_read, 1, 0))

    def advance(carried, block_item):
        memory, prefix = carried
        transition, addition, reading, intra_out = block_item
        emitted = intra_out + contract("hvn,hnt->hvt", memory, reading)
        weighted = contract("han,hnt->hat", prefix, reading)
        memory = contract("hvn,hnk->hvk", memory, transition) + addition
        prefix = contract("han,hnk->hak", prefix, transition)
        return ((memory, prefix), (emitted, weighted))

    (slab_state, slab_trans), (emitted, weighted) = lax.scan(
        advance, (empty_state, identity), (trans_seq, state_seq, start_read, local_out)
    )
    arriving = incoming_state(slab_trans, slab_state)
    outputs = emitted + contract("hva,chat->chvt", arriving, weighted)
    read_blk = jnp.moveaxis(outputs, 0, 1)
    centre = jnp.mean(read_blk, axis=2, keepdims=True)
    centred = read_blk - centre
    spread = jnp.mean(centred * centred, axis=2, keepdims=True)
    standardised = centred * lax.rsqrt(spread + 0.00064) * cluster_multiplier.reshape(
        owned_units, 1, UNIT_CHANNELS, 1
    ) + cluster_offset.reshape(owned_units, 1, UNIT_CHANNELS, 1)
    reward_addend = (
        jnp.sum(
            acceptance_segment
            * address_segment
            * reward_coefficient.reshape(owned_units, 1, UNIT_CHANNELS, 1),
            axis=2,
            keepdims=True,
        )
        * value_blk
    )
    blended_segment = (standardised + reward_addend) * divided_segments(
        emission_valve, owned_units, owned_segments
    )
    blended_content = (
        jnp.transpose(blended_segment, (0, 2, 1, 3)).reshape(channels, length).astype(jnp.bfloat16)
    )
    own_rows = lax.all_to_all(projection_weights, "head", split_axis=0, concat_axis=1, tiled=True)
    projected = jnp.dot(
        own_rows,
        lax.all_gather(blended_content, "head", axis=0, tiled=True),
        preferred_element_type=jnp.float32,
    )
    return (projected + skip_stream.astype(jnp.float32)).astype(jnp.bfloat16)


def solution(mesh):
    in_specs = (
        P("head", "seq"),
        P("head", "seq"),
        P("head", "seq"),
        P("head", "seq"),
        P("head", "seq"),
        P("head", "seq"),
        P("head", "seq"),
        P("head"),
        P("head"),
        P("head"),
        P("head"),
        P(None, "head"),
    )
    out_specs = P("head", "seq")
    return jax.shard_map(
        on_device, mesh=mesh, in_specs=in_specs, out_specs=out_specs, check_vma=False
    )
```

profile of v0, /device:TPU:0, one launch (start us, length us, event | category | flops | bytes accessed | tf_op | source)
XLA Modules:
  0.0 269.2 jit_solution(17037903070430067817)
XLA Ops:
  6.5 5.8 %all-to-all-start = ((bf16[4,1024,1024]{2,1,0:T(8,128)(2,1)}), bf16[4,1024,1024]{2,1,0:T(8,128)(2,1)}, u32[]{:S(2)}, u32[]{:S(2)}) async-start(bf16[4,1024,1024]{2,1,0:T(8,128)(2,1)} %bitcast.223), calls=%async_computation | async-start | bytes 16777216 | tf_op jit(solution)/shard_map/all_to_all | solution.py:148
  14.5 7.5 %reduce_window_sum.11 = f32[16,2,64,64]{3,2,1,0:T(8,128)S(1)} reduce-window(f32[16,2,64,64]{3,2,1,0:T(8,128)S(1)} %bitcast.225, f32[]{:T(128)} %constant.30.clone.1), window={size=1x1x1x64 pad=0_0x0_0x0_0x63_0}, to_apply=%region_0.0 | reduce-window | flops 8257536 | bytes 1048580 | tf_op jit(solution)/shard_map/jit(cumsum)/reduce_window_sum | solution.py:71
  31.5 2.7 copy.193
  36.3 2.9 %convolution_multiply_fusion.3 = f32[16,2,64,64]{3,2,1,0:T(8,128)} fusion(f32[16,2,64,64]{2,3,1,0:T(8,128)S(1)} %get-tuple-element.195, f32[64,64]{1,0:T(8,128)S(1)} %fusion.59, f32[16,64,2,64]{1,3,2,0:T(8,128)S(1)} %copy.182, f32[16,2,64,64]{2,3,1,0:T(8,128)S(1)} %copy.186), kind=kOutput, calls=%fused_computation.49 | convolution fusion | flops 101056512 | bytes 2113536 | tf_op jit(solution)/shard_map/hcns,hcnt->hcst/dot_general | solution.py:20
  39.2 2.9 %convolution_multiply_fusion.2 = f32[16,2,64,64]{3,2,1,0:T(8,128)} fusion(f32[16,2,64,64]{2,3,1,0:T(8,128)S(1)} %get-tuple-element.195, f32[64,64]{1,0:T(8,128)S(1)} %fusion.59, f32[16,2,64,64]{2,3,1,0:T(8,128)S(1)} %get-tuple-element.194, f32[16,2,64,64]{2,3,1,0:T(8,128)S(1)} %copy.186), kind=kOutput, calls=%fused_computation.48 | convolution fusion | flops 101056512 | bytes 2113536 | tf_op jit(solution)/shard_map/hcns,hcnt->hcst/dot_general | solution.py:20
  42.1 3.0 %convolution_multiply_fusion.1 = f32[16,2,64,64]{3,2,1,0:T(8,128)} fusion(f32[64,64]{1,0:T(8,128)S(1)} %fusion.60, f32[16,64,2,64]{1,3,2,0:T(8,128)S(1)} %copy.213, f32[16,2,64,64]{2,3,1,0:T(8,128)S(1)} %copy.186, f32[16,2,64,64]{2,3,1,0:T(8,128)S(1)} %get-tuple-element.194), kind=kOutput, calls=%fused_computation.43 | convolution fusion | flops 101187584 | bytes 2113536 | tf_op jit(solution)/shard_map/hcns,hcnt->hcst/dot_general | solution.py:20
  45.1 3.0 %convolution_multiply_fusion = f32[16,2,64,64]{3,2,1,0:T(8,128)} fusion(f32[64,64]{1,0:T(8,128)S(1)} %fusion.60, f32[16,64,2,64]{1,3,2,0:T(8,128)S(1)} %copy.213, f32[16,2,64,64]{2,3,1,0:T(8,128)S(1)} %copy.186, f32[16,64,2,64]{1,3,2,0:T(8,128)S(1)} %copy.182), kind=kOutput, calls=%fused_computation.40 | convolution fusion | flops 101187584 | bytes 2113536 | tf_op jit(solution)/shard_map/hcns,hcnt->hcst/dot_general | solution.py:20
  61.5 3.7 %convolution_add_fusion.6 = f32[16,2,128,64]{2,3,1,0:T(8,128)S(1)} fusion(f32[16,2,64,64]{3,2,1,0:T(8,128)} %convolution_multiply_fusion.2, f32[16,2,64,64]{2,3,1,0:T(8,128)} %copy-done.3, f32[16,2,64,64]{2,3,1,0:T(8,128)S(1)} %convolution_bitcast_fusion.11), kind=kOutput, calls=%fused_computation.37 | convolution fusion | flops 201850880 | bytes 2621440 | tf_op jit(solution)/shard_map/hcrs,hcst->hcrt/dot_general | solution.py:20
  80.5 3.1 %fusion.24 = f32[2,16,64,64]{2,3,0,1:T(8,128)} fusion(f32[16,2,64,64]{3,2,1,0:T(8,128)S(1)} %copy-done.4, f32[16,64,2,64]{1,3,2,0:T(8,128)S(1)} %copy.213, f32[16,2,128,64]{2,3,1,0:T(8,128)S(1)} %convolution_add_fusion.1, f32[16,2,64,64]{2,3,1,0:T(8,128)S(1)} %copy.186), kind=kOutput, calls=%fused_computation.39 | convolution fusion | flops 100925440 | bytes 3145728 | tf_op jit(solution)/shard_map/hcns,hcst->hcnt/dot_general | solution.py:20
  83.6 3.0 %fusion.25 = f32[2,16,64,64]{3,2,0,1:T(8,128)} fusion(f32[2,16,64,64]{3,2,0,1:T(8,128)S(1)} %convolution_bitcast_fusion.9, f32[16,2,64,64]{3,2,1,0:T(8,128)S(1)} %copy-done.4, f32[16,2,128,64]{2,3,1,0:T(8,128)S(1)} %convolution_add_fusion.1), kind=kOutput, calls=%fused_computation.42 | convolution fusion | flops 100794368 | bytes 2621440 | tf_op jit(solution)/shard_map/hcvs,hcst->hcvt/dot_general | solution.py:20
  90.2 4.6 %fusion.26 = f32[2,16,64,64]{3,2,0,1:T(8,128)} fusion(f32[2,16,64,64]{3,2,0,1:T(8,128)S(1)} %convolution_bitcast_fusion.10, f32[16,2,128,64]{2,3,1,0:T(8,128)} %copy-done, f32[16,2,64,64]{2,3,1,0:T(8,128)} %copy-done.2, f32[16,2,64,64]{2,3,1,0:T(8,128)S(1)} %copy.186, f32[16,2,64]{2,1,0:T(2,128)S(1)} %copy.202), kind=kOutput, calls=%fused_computation.45 | convolution fusion | flops 101056512 | bytes 3153920 | tf_op jit(solution)/shard_map/hcvs,hcks->hcvk/dot_general | solution.py:20
  94.9 3.6 %fusion.27 = f32[2,16,64,64]{3,2,0,1:T(8,128)S(1)} fusion(f32[16,2,128,64]{2,3,1,0:T(8,128)S(1)} %copy-done.1, f32[2,16,64]{2,0,1:T(2,128)S(1)} %copy.206, f32[64,64]{1,0:T(8,128)S(1)} %fusion.58, f32[16,2,64,64]{2,3,1,0:T(8,128)} %copy-done.2, f32[16,2,64,64]{2,3,1,0:T(8,128)S(1)} %copy.186, f32[16,2,64]{2,1,0:T(2,128)S(1)} %copy.202), kind=kOutput, calls=%fused_computation.47 | convolution fusion | flops 101187584 | bytes 2654208 | tf_op jit(solution)/shard_map/hcns,hcks->hcnk/dot_general | solution.py:20
  98.5 23.8 %while.28 = (s32[]{:T(128)}, f32[16,64,64]{1,2,0:T(8,128)}, f32[16,64,64]{1,2,0:T(8,128)S(1)}, f32[2,16,64,64]{3,2,0,1:T(8,128)}, f32[2,16,64,64]{2,3,0,1:T(8,12...) while((s32[]{:T(128)}, f32[16,64,64]{1,2,0:T(8,128)}, ...), condition=%wide.region_3.4_spmd.clone, body=%wide.region_2.3_spmd.clone.sunk | while | flops 201588736 | bytes 10487940 | solution.py:120
  124.6 103.7 %while.27 = (s32[]{:T(128)}, f32[16,64,64]{2,1,0:T(8,128)S(1)}, f32[16,64,64]{2,1,0:T(8,128)S(1)}, f32[16,64,64]{2,1,0:T(8,128)S(1)}, s32[]{:T(128)}) while((s32[]{:T(128)}, f32[16,64,64]{2,1,0:T(8,128)S(1)}, f32[16,64,64]{2,1,0:T(8,128)S(1)}, f32[16,64,64]{2,1,0:T(8,128)S(1)}, s32[]{:T(128)}) %tuple.52), condition=%wide.region_5.6_spmd, body=%wide.region_4.5_spmd.sunk | while | flops 50397184 | bytes 2097253 | solution.py:43
  125.3 4.9 %collective-permute-start = (f32[16,64,64]{2,1,0:T(8,128)S(1)}, f32[16,64,64]{2,1,0:T(8,128)S(1)}, u32[]{:S(2)}, u32[]{:S(2)}) collective-permute-start(f32[16,64,64]{2,1,0:T(8,128)S(1)} %convolution_add_fusion.8), channel_id=1, source_target_pairs={{0,1},{1,2},{2,3},{3,4},{4,5},{5,6},{6,7},{8,9},{9,10},{10,11},{11... | collective-permute-start | bytes 786440 | tf_op jit(solution)/shard_map/while/body/eval_jaxpr/ppermute | solution.py:16
  130.2 11.7 %collective-permute-done = f32[16,64,64]{2,1,0:T(8,128)S(1)} collective-permute-done((f32[16,64,64]{2,1,0:T(8,128)S(1)}, f32[16,64,64]{2,1,0:T(8,128)S(1)}, u32[]{:S(2)}, u32[]{:S(2)}) %collective-permute-start) | collective-permute-done | bytes 262176 | tf_op jit(solution)/shard_map/while/body/eval_jaxpr/ppermute | solution.py:16
  142.6 4.4 %collective-permute-start = (f32[16,64,64]{2,1,0:T(8,128)S(1)}, f32[16,64,64]{2,1,0:T(8,128)S(1)}, u32[]{:S(2)}, u32[]{:S(2)}) collective-permute-start(f32[16,64,64]{2,1,0:T(8,128)S(1)} %convolution_add_fusion.8), channel_id=1, source_target_pairs={{0,1},{1,2},{2,3},{3,4},{4,5},{5,6},{6,7},{8,9},{9,10},{10,11},{11... | collective-permute-start | bytes 786440 | tf_op jit(solution)/shard_map/while/body/eval_jaxpr/ppermute | solution.py:16
  147.0 10.9 %collective-permute-done = f32[16,64,64]{2,1,0:T(8,128)S(1)} collective-permute-done((f32[16,64,64]{2,1,0:T(8,128)S(1)}, f32[16,64,64]{2,1,0:T(8,128)S(1)}, u32[]{:S(2)}, u32[]{:S(2)}) %collective-permute-start) | collective-permute-done | bytes 262176 | tf_op jit(solution)/shard_map/while/body/eval_jaxpr/ppermute | solution.py:16
  158.5 4.4 %collective-permute-start = (f32[16,64,64]{2,1,0:T(8,128)S(1)}, f32[16,64,64]{2,1,0:T(8,128)S(1)}, u32[]{:S(2)}, u32[]{:S(2)}) collective-permute-start(f32[16,64,64]{2,1,0:T(8,128)S(1)} %convolution_add_fusion.8), channel_id=1, source_target_pairs={{0,1},{1,2},{2,3},{3,4},{4,5},{5,6},{6,7},{8,9},{9,10},{10,11},{11... | collective-permute-start | bytes 786440 | tf_op jit(solution)/shard_map/while/body/eval_jaxpr/ppermute | solution.py:16
  163.0 10.0 %collective-permute-done = f32[16,64,64]{2,1,0:T(8,128)S(1)} collective-permute-done((f32[16,64,64]{2,1,0:T(8,128)S(1)}, f32[16,64,64]{2,1,0:T(8,128)S(1)}, u32[]{:S(2)}, u32[]{:S(2)}) %collective-permute-start) | collective-permute-done | bytes 262176 | tf_op jit(solution)/shard_map/while/body/eval_jaxpr/ppermute | solution.py:16
  173.6 5.3 %collective-permute-start = (f32[16,64,64]{2,1,0:T(8,128)S(1)}, f32[16,64,64]{2,1,0:T(8,128)S(1)}, u32[]{:S(2)}, u32[]{:S(2)}) collective-permute-start(f32[16,64,64]{2,1,0:T(8,128)S(1)} %convolution_add_fusion.8), channel_id=1, source_target_pairs={{0,1},{1,2},{2,3},{3,4},{4,5},{5,6},{6,7},{8,9},{9,10},{10,11},{11... | collective-permute-start | bytes 786440 | tf_op jit(solution)/shard_map/while/body/eval_jaxpr/ppermute | solution.py:16
  178.9 9.1 %collective-permute-done = f32[16,64,64]{2,1,0:T(8,128)S(1)} collective-permute-done((f32[16,64,64]{2,1,0:T(8,128)S(1)}, f32[16,64,64]{2,1,0:T(8,128)S(1)}, u32[]{:S(2)}, u32[]{:S(2)}) %collective-permute-start) | collective-permute-done | bytes 262176 | tf_op jit(solution)/shard_map/while/body/eval_jaxpr/ppermute | solution.py:16
  188.7 5.3 %collective-permute-start = (f32[16,64,64]{2,1,0:T(8,128)S(1)}, f32[16,64,64]{2,1,0:T(8,128)S(1)}, u32[]{:S(2)}, u32[]{:S(2)}) collective-permute-start(f32[16,64,64]{2,1,0:T(8,128)S(1)} %convolution_add_fusion.8), channel_id=1, source_target_pairs={{0,1},{1,2},{2,3},{3,4},{4,5},{5,6},{6,7},{8,9},{9,10},{10,11},{11... | collective-permute-start | bytes 786440 | tf_op jit(solution)/shard_map/while/body/eval_jaxpr/ppermute | solution.py:16
  194.0 8.3 %collective-permute-done = f32[16,64,64]{2,1,0:T(8,128)S(1)} collective-permute-done((f32[16,64,64]{2,1,0:T(8,128)S(1)}, f32[16,64,64]{2,1,0:T(8,128)S(1)}, u32[]{:S(2)}, u32[]{:S(2)}) %collective-permute-start) | collective-permute-done | bytes 262176 | tf_op jit(solution)/shard_map/while/body/eval_jaxpr/ppermute | solution.py:16
  203.0 5.3 %collective-permute-start = (f32[16,64,64]{2,1,0:T(8,128)S(1)}, f32[16,64,64]{2,1,0:T(8,128)S(1)}, u32[]{:S(2)}, u32[]{:S(2)}) collective-permute-start(f32[16,64,64]{2,1,0:T(8,128)S(1)} %convolution_add_fusion.8), channel_id=1, source_target_pairs={{0,1},{1,2},{2,3},{3,4},{4,5},{5,6},{6,7},{8,9},{9,10},{10,11},{11... | collective-permute-start | bytes 786440 | tf_op jit(solution)/shard_map/while/body/eval_jaxpr/ppermute | solution.py:16
  208.3 7.4 %collective-permute-done = f32[16,64,64]{2,1,0:T(8,128)S(1)} collective-permute-done((f32[16,64,64]{2,1,0:T(8,128)S(1)}, f32[16,64,64]{2,1,0:T(8,128)S(1)}, u32[]{:S(2)}, u32[]{:S(2)}) %collective-permute-start) | collective-permute-done | bytes 262176 | tf_op jit(solution)/shard_map/while/body/eval_jaxpr/ppermute | solution.py:16
  216.4 5.3 %collective-permute-start = (f32[16,64,64]{2,1,0:T(8,128)S(1)}, f32[16,64,64]{2,1,0:T(8,128)S(1)}, u32[]{:S(2)}, u32[]{:S(2)}) collective-permute-start(f32[16,64,64]{2,1,0:T(8,128)S(1)} %convolution_add_fusion.8), channel_id=1, source_target_pairs={{0,1},{1,2},{2,3},{3,4},{4,5},{5,6},{6,7},{8,9},{9,10},{10,11},{11... | collective-permute-start | bytes 786440 | tf_op jit(solution)/shard_map/while/body/eval_jaxpr/ppermute | solution.py:16
  221.7 6.6 %collective-permute-done = f32[16,64,64]{2,1,0:T(8,128)S(1)} collective-permute-done((f32[16,64,64]{2,1,0:T(8,128)S(1)}, f32[16,64,64]{2,1,0:T(8,128)S(1)}, u32[]{:S(2)}, u32[]{:S(2)}) %collective-permute-start) | collective-permute-done | bytes 262176 | tf_op jit(solution)/shard_map/while/body/eval_jaxpr/ppermute | solution.py:16
  228.3 4.7 %bitcast_reduce_fusion = (f32[16,2,64]{2,1,0:T(2,128)S(1)}, f32[2,16,64,64]{3,2,0,1:T(8,128)S(1)}) fusion(f32[2,16,64,64]{3,2,0,1:T(8,128)} %get-tuple-element.77, f32[2,16,64,64]{2,3,0,1:T(8,128)} %get-tuple-element.78, f32[16,64,64]{2,1,0:T(8,128)S(1)} %get-tuple-element.81), kind=kOutput, calls=%fused_computation.64 | convolution fusion | flops 100923392 | bytes 1843200 | tf_op jit(solution)/shard_map/hva,chat->chvt/dot_general | solution.py:20
  236.6 11.5 %copy.236 = bf16[1024,4,1024]{0,2,1:T(8,128)(2,1)} copy(bf16[1024,4,1024]{2,0,1:T(8,128)(2,1)} %bitcast.24) | data formatting | bytes 16777216 | tf_op jit(solution)/shard_map/all_to_all | solution.py:148
  248.0 8.3 %all-gather.2.cloned.1.call-done = bf16[4096,128]{0,1:T(8,128)(2,1)} async-done(((bf16[1024,128]{0,1:T(8,128)(2,1)}), bf16[4096,128]{0,1:T(8,128)(2,1)}) %all-gather.2.cloned.1.call-update) | async-done | bytes 1048592 | tf_op jit(solution)/shard_map/all_gather | solution.py:151
  256.3 5.0 %fusion.30 = bf16[1024,128]{0,1:T(8,128)(2,1)S(1)} fusion(bf16[4096,128]{0,1:T(8,128)(2,1)} %all-gather.2.cloned.1.call-done, bf16[1024,4096]{0,1:T(8,128)(2,1)} %bitcast.222, bf16[1024,128]{0,1:T(8,128)(2,1)S(1)} %copy.237), kind=kOutput, calls=%fused_computation.57 | convolution fusion | flops 1074135040 | bytes 9961472 | tf_op jit(solution)/shard_map/dot_general | solution.py:149
  (124 shorter events, 80.6 us)
Async XLA Ops:
  6.5 5.9 %copy-start.9 = (bf16[1024,128]{1,0:T(8,128)(2,1)S(1)}, bf16[1024,128]{1,0:T(8,128)(2,1)}, u32[]{:S(2)}) copy-start(bf16[1024,128]{1,0:T(8,128)(2,1)} %param.21) | copy-start | bytes 786436
  6.5 230.0 %all-to-all-start = ((bf16[4,1024,1024]{2,1,0:T(8,128)(2,1)}), bf16[4,1024,1024]{2,1,0:T(8,128)(2,1)}, u32[]{:S(2)}, u32[]{:S(2)}) async-start(bf16[4,1024,1024]{2,1,0:T(8,128)(2,1)} %bitcast.223), calls=%async_computation | async-start | bytes 16777216 | tf_op jit(solution)/shard_map/all_to_all | solution.py:148
  12.3 10.7 %copy-start.10 = (bf16[1024,128]{1,0:T(8,128)(2,1)S(1)}, bf16[1024,128]{1,0:T(8,128)(2,1)}, u32[]{:S(2)}) copy-start(bf16[1024,128]{1,0:T(8,128)(2,1)} %param.18) | copy-start | bytes 786436
  12.3 15.8 %copy-start.13 = (f32[1024]{0:T(1024)S(1)}, f32[1024]{0:T(1024)}, u32[]{:S(2)}) copy-start(f32[1024]{0:T(1024)} %param.23) | copy-start | bytes 12292
  12.3 15.9 %copy-start.14 = (f32[1024]{0:T(1024)S(1)}, f32[1024]{0:T(1024)}, u32[]{:S(2)}) copy-start(f32[1024]{0:T(1024)} %param.24) | copy-start | bytes 12292
  12.4 244.0 %all-gather.2.cloned.1.call-start = ((), (), s32[]{:S(2)}) async-start(), calls=%async_computation.1 | async-start | bytes 1310720 | tf_op jit(solution)/shard_map/all_gather | solution.py:151
  22.0 1.0 copy-start.5
  36.3 11.8 %copy-start.2 = (f32[16,2,64,64]{2,3,1,0:T(8,128)}, f32[16,2,64,64]{2,3,1,0:T(8,128)S(1)}, u32[]{:S(2)}) copy-start(f32[16,2,64,64]{2,3,1,0:T(8,128)S(1)} %get-tuple-element.194) | copy-start | bytes 1572868
  36.3 11.8 %copy-start.3 = (f32[16,2,64,64]{2,3,1,0:T(8,128)}, f32[16,2,64,64]{2,3,1,0:T(8,128)S(1)}, u32[]{:S(2)}) copy-start(f32[16,2,64,64]{2,3,1,0:T(8,128)S(1)} %get-tuple-element.195) | copy-start | bytes 1572868
  39.2 8.9 %copy-start.6 = (f32[16,2,64,64]{3,2,1,0:T(8,128)S(1)}, f32[16,2,64,64]{3,2,1,0:T(8,128)}, u32[]{:S(2)}) copy-start(f32[16,2,64,64]{3,2,1,0:T(8,128)} %copy-done.5) | copy-start | bytes 1572868
  69.5 9.2 %copy-start.7 = (bf16[16,2,64,64]{3,2,1,0:T(8,128)(2,1)S(1)}, bf16[16,2,64,64]{3,2,1,0:T(8,128)(2,1)}, u32[]{:S(2)}) copy-start(bf16[16,2,64,64]{3,2,1,0:T(8,128)(2,1)} %copy.191) | copy-start | bytes 786436
  69.5 9.2 %copy-start.8 = (f32[16,2,64,64]{3,2,1,0:T(8,128)S(1)}, f32[16,2,64,64]{3,2,1,0:T(8,128)}, u32[]{:S(2)}) copy-start(f32[16,2,64,64]{3,2,1,0:T(8,128)} %convolution_multiply_fusion) | copy-start | bytes 1572868
  72.6 7.9 %copy-start.4 = (f32[16,2,64,64]{3,2,1,0:T(8,128)S(1)}, f32[16,2,64,64]{3,2,1,0:T(8,128)}, u32[]{:S(2)}) copy-start(f32[16,2,64,64]{3,2,1,0:T(8,128)} %convolution_multiply_fusion.1) | copy-start | bytes 1572868
  80.5 3.1 %copy-start = (f32[16,2,128,64]{2,3,1,0:T(8,128)}, f32[16,2,128,64]{2,3,1,0:T(8,128)S(1)}, u32[]{:S(2)}) copy-start(f32[16,2,128,64]{2,3,1,0:T(8,128)S(1)} %convolution_add_fusion.1) | copy-start | bytes 3145732
  86.6 8.3 %copy-start.1 = (f32[16,2,128,64]{2,3,1,0:T(8,128)S(1)}, f32[16,2,128,64]{2,3,1,0:T(8,128)}, u32[]{:S(2)}) copy-start(f32[16,2,128,64]{2,3,1,0:T(8,128)} %copy-done) | copy-start | bytes 3145732
  98.5 25.3 %copy-start.11 = (bf16[1024,128]{1,0:T(8,128)(2,1)S(1)}, bf16[1024,128]{1,0:T(8,128)(2,1)}, u32[]{:S(2)}) copy-start(bf16[1024,128]{1,0:T(8,128)(2,1)} %param.20) | copy-start | bytes 786436
  98.5 25.9 %copy-start.15 = (f32[1024]{0:T(1024)S(1)}, f32[1024]{0:T(1024)}, u32[]{:S(2)}) copy-start(f32[1024]{0:T(1024)} %param.26) | copy-start | bytes 12292
  98.5 26.0 %copy-start.16 = (f32[1024]{0:T(1024)S(1)}, f32[1024]{0:T(1024)}, u32[]{:S(2)}) copy-start(f32[1024]{0:T(1024)} %param.25) | copy-start | bytes 12292
  124.6 111.8 %copy-start.12 = (bf16[1024,128]{1,0:T(8,128)(2,1)S(1)}, bf16[1024,128]{1,0:T(8,128)(2,1)}, u32[]{:S(2)}) copy-start(bf16[1024,128]{1,0:T(8,128)(2,1)} %param.16) | copy-start | bytes 786436
  125.3 16.7 %collective-permute-start = (f32[16,64,64]{2,1,0:T(8,128)S(1)}, f32[16,64,64]{2,1,0:T(8,128)S(1)}, u32[]{:S(2)}, u32[]{:S(2)}) collective-permute-start(f32[16,64,64]{2,1,0:T(8,128)S(1)} %convolution_add_fusion.8), channel_id=1, source_target_pairs={{0,1},{1,2},{2,3},{3,4},{4,5},{5,6},{6,7},{8,9},{9,10},{10,11},{11... | collective-permute-start | bytes 786440 | tf_op jit(solution)/shard_map/while/body/eval_jaxpr/ppermute | solution.py:16
  142.6 15.3 %collective-permute-start = (f32[16,64,64]{2,1,0:T(8,128)S(1)}, f32[16,64,64]{2,1,0:T(8,128)S(1)}, u32[]{:S(2)}, u32[]{:S(2)}) collective-permute-start(f32[16,64,64]{2,1,0:T(8,128)S(1)} %convolution_add_fusion.8), channel_id=1, source_target_pairs={{0,1},{1,2},{2,3},{3,4},{4,5},{5,6},{6,7},{8,9},{9,10},{10,11},{11... | collective-permute-start | bytes 786440 | tf_op jit(solution)/shard_map/while/body/eval_jaxpr/ppermute | solution.py:16
  158.5 14.4 %collective-permute-start = (f32[16,64,64]{2,1,0:T(8,128)S(1)}, f32[16,64,64]{2,1,0:T(8,128)S(1)}, u32[]{:S(2)}, u32[]{:S(2)}) collective-permute-start(f32[16,64,64]{2,1,0:T(8,128)S(1)} %convolution_add_fusion.8), channel_id=1, source_target_pairs={{0,1},{1,2},{2,3},{3,4},{4,5},{5,6},{6,7},{8,9},{9,10},{10,11},{11... | collective-permute-start | bytes 786440 | tf_op jit(solution)/shard_map/while/body/eval_jaxpr/ppermute | solution.py:16
  173.6 14.4 %collective-permute-start = (f32[16,64,64]{2,1,0:T(8,128)S(1)}, f32[16,64,64]{2,1,0:T(8,128)S(1)}, u32[]{:S(2)}, u32[]{:S(2)}) collective-permute-start(f32[16,64,64]{2,1,0:T(8,128)S(1)} %convolution_add_fusion.8), channel_id=1, source_target_pairs={{0,1},{1,2},{2,3},{3,4},{4,5},{5,6},{6,7},{8,9},{9,10},{10,11},{11... | collective-permute-start | bytes 786440 | tf_op jit(solution)/shard_map/while/body/eval_jaxpr/ppermute | solution.py:16
  188.7 13.6 %collective-permute-start = (f32[16,64,64]{2,1,0:T(8,128)S(1)}, f32[16,64,64]{2,1,0:T(8,128)S(1)}, u32[]{:S(2)}, u32[]{:S(2)}) collective-permute-start(f32[16,64,64]{2,1,0:T(8,128)S(1)} %convolution_add_fusion.8), channel_id=1, source_target_pairs={{0,1},{1,2},{2,3},{3,4},{4,5},{5,6},{6,7},{8,9},{9,10},{10,11},{11... | collective-permute-start | bytes 786440 | tf_op jit(solution)/shard_map/while/body/eval_jaxpr/ppermute | solution.py:16
  203.0 12.8 %collective-permute-start = (f32[16,64,64]{2,1,0:T(8,128)S(1)}, f32[16,64,64]{2,1,0:T(8,128)S(1)}, u32[]{:S(2)}, u32[]{:S(2)}) collective-permute-start(f32[16,64,64]{2,1,0:T(8,128)S(1)} %convolution_add_fusion.8), channel_id=1, source_target_pairs={{0,1},{1,2},{2,3},{3,4},{4,5},{5,6},{6,7},{8,9},{9,10},{10,11},{11... | collective-permute-start | bytes 786440 | tf_op jit(solution)/shard_map/while/body/eval_jaxpr/ppermute | solution.py:16
  216.4 12.0 %collective-permute-start = (f32[16,64,64]{2,1,0:T(8,128)S(1)}, f32[16,64,64]{2,1,0:T(8,128)S(1)}, u32[]{:S(2)}, u32[]{:S(2)}) collective-permute-start(f32[16,64,64]{2,1,0:T(8,128)S(1)} %convolution_add_fusion.8), channel_id=1, source_target_pairs={{0,1},{1,2},{2,3},{3,4},{4,5},{5,6},{6,7},{8,9},{9,10},{10,11},{11... | collective-permute-start | bytes 786440 | tf_op jit(solution)/shard_map/while/body/eval_jaxpr/ppermute | solution.py:16
Sparse Core Ops, SparseCore 0:
  236.5 19.7 all-gather.1
where the time goes:
time: 274 us; the launch traced here: 269 us
  matrix products  80.2 us (29%)
  waiting for transfers between devices  72.4 us (26%)
  local copies, waits for them, and re-layouts  49.2 us (18%)
  starting transfers between devices  40.8 us (15%)
  between operations  14.1 us (5%)
  other arithmetic  12.1 us (4%)
    dot_general x38, matrix products, contract(): return jnp.einsum(form, left, right, precision=HIGHEST)  75.3 us
    ppermute x7, waiting for transfers between devices, from_behind(): return lax.ppermute(block, axis, route)  64.1 us
    ppermute x7, starting transfers between devices, from_behind(): return lax.ppermute(block, axis, route)  35 us
    all_to_all x1, local copies, waits for them, and re-layouts, on_device(): lax.all_to_all(projection_weights, 'head', split_axis=0, concat_axis=1, t...  11.5 us
    transpose x8, local copies, waits for them, and re-layouts, divided_segments(): jnp.transpose(field.astype(jnp.float32).reshape(owned_units, UNIT_CHANNEL...  10.7 us
    all_gather x1, waiting for transfers between devices, on_device(): lax.all_gather(blended_content, 'head', axis=0, tiled=True)  8.3 us
    reshape x5, local copies, waits for them, and re-layouts, divided_segments(): field.astype(jnp.float32)  8 us
    another operation x1, other arithmetic, on_device(): running = jnp.cumsum(decay_blk, axis=3)  7.52 us
  transfers between devices with their start and end apart: 9, of which 8 were waited for; matrix products, arithmetic and copies ran while one was open for 50% of the time, Pallas kernels for 0%

commit v1 on v0

v1 whole, which is shorter than its diff:
```python
import functools

import jax
import jax.numpy as jnp
from jax import lax
from jax.experimental import pallas as pl
from jax.experimental.pallas import tpu as pltpu
from jax.sharding import PartitionSpec as P

MESH = pl.DeviceIdType.MESH
UNIT = 64
GROUP = 4
F32 = jnp.float32
BF16 = jnp.bfloat16


def split(x):
    hi = x.astype(BF16)
    return hi, (x - hi.astype(F32)).astype(BF16)


def mm(a, b, ca=1, cb=0, passes=3):
    dims = (((ca,), (cb,)), ((), ()))
    if passes == 1:
        return lax.dot_general(a.astype(BF16), b.astype(BF16), dims, preferred_element_type=F32)
    if a.dtype == BF16:
        bh, bl = split(b)
        a2 = jnp.concatenate([a, a], axis=ca)
        b2 = jnp.concatenate([bh, bl], axis=cb)
        return lax.dot_general(a2, b2, dims, preferred_element_type=F32)
    ah, al = split(a)
    bh, bl = split(b)
    a3 = jnp.concatenate([ah, ah, al], axis=ca)
    b3 = jnp.concatenate([bh, bl, bh], axis=cb)
    return lax.dot_general(a3, b3, dims, preferred_element_type=F32)


def columns_of(row_ref, first, count):
    i = lax.broadcasted_iota(jnp.int32, (128, 128), 0)
    j = lax.broadcasted_iota(jnp.int32, (128, 128), 1)
    eye = i == j
    out = []
    for n in range(count):
        row = row_ref[pl.ds(first + n, 1), :]
        out.append(jnp.sum(jnp.where(eye, jnp.broadcast_to(row, (128, 128)), 0.0), axis=1, keepdims=True))
    return jnp.concatenate(out, axis=0) if count > 1 else out[0]


def local_kernel(r_ref, k_ref, v_ref, w_ref, a_ref, er_ref, tp_ref, loc_ref, st_ref):
    length = r_ref.shape[1]
    mid_at = length // 2 - 1
    si = lax.broadcasted_iota(jnp.int32, (length, length), 0)
    ti = lax.broadcasted_iota(jnp.int32, (length, length), 1)
    ones = jnp.where(si <= ti, 1.0, 0.0) - jnp.where(si <= mid_at, 1.0, 0.0)
    w16 = w_ref[...]
    c = jnp.dot(w16, ones.astype(BF16), preferred_element_type=F32)
    w = w16.astype(F32)
    er = columns_of(er_ref, pl.program_id(0) * (GROUP // 2), GROUP // 2)
    k = k_ref[...].astype(F32)
    scaled = k * er
    heads = range(GROUP)
    sl = [slice(h * UNIT, (h + 1) * UNIT) for h in heads]
    kk = jnp.concatenate(
        [scaled[s] * lax.rsqrt(jnp.sum(scaled[s] * scaled[s], axis=0, keepdims=True) + 1e-06) for s in sl], axis=0
    )
    back = jnp.exp(-c)
    pulled_back = a_ref[...].astype(F32) * kk * back
    keys_back = k * back
    removal = -kk * jnp.exp(c - w)
    recept = r_ref[...].astype(F32) * jnp.exp(c)
    emid = jnp.exp(w[:, 0:1] - c[:, 0:1])
    eend = jnp.exp(c[:, length - 1 :])
    etot = emid * eend
    pulled_end = pulled_back * eend
    keys_end = keys_back * eend

    before = si < ti
    upto = si <= ti
    mix = [
        mm(
            jnp.concatenate([pulled_back[s], keys_back[s]], axis=1),
            jnp.concatenate([removal[s], recept[s]], axis=1),
            0,
            0,
        )
        for s in sl
    ]
    pair_mix = [jnp.where(before, m[:length, :length], 0.0) for m in mix]
    key_mix = [jnp.where(before, m[length:, :length], 0.0) for m in mix]
    pair_read = [jnp.where(upto, m[:length, length:], 0.0) for m in mix]
    key_read = [jnp.where(upto, m[length:, length:], 0.0) for m in mix]
    eye = jnp.where(si == ti, 1.0, 0.0)
    size = 1
    inv = None
    while size < length:
        joins = (si // (2 * size) == ti // (2 * size)) & (si // size != ti // size)
        off = [jnp.where(joins, m, 0.0) for m in pair_mix]
        if inv is None:
            inv = [eye + o for o in off]
        else:
            half = [mm(n, o) for n, o in zip(inv, off)]
            inv = [n + mm(x, n) for n, x in zip(inv, half)]
        size *= 2
    v16 = v_ref[...]
    vk = [mm(v16[s], m) for s, m in zip(sl, key_mix)]
    solved = [mm(jnp.concatenate([x, removal[s]], axis=0), n) for x, s, n in zip(vk, sl, inv)]
    solved = [jnp.concatenate([x[:UNIT], x[UNIT:] * emid[s]], axis=0) for x, s in zip(solved, sl)]
    ends = [mm(x, pulled_end[s], 1, 1) for x, s in zip(solved, sl)]
    vke = [mm(v16[s], keys_end[s], 1, 1) for s in sl]
    reads = [mm(x, p) for x, p in zip(solved, pair_read)]
    vkr = [mm(v16[s], m) for s, m in zip(sl, key_read)]
    diag = lax.broadcasted_iota(jnp.int32, (UNIT, UNIT), 0) == lax.broadcasted_iota(jnp.int32, (UNIT, UNIT), 1)
    for h in heads:
        s = sl[h]
        trans = ends[h][UNIT:] + jnp.where(diag, jnp.broadcast_to(etot[s], (UNIT, UNIT)), 0.0)
        tp_ref[s, :] = jnp.concatenate([trans, ends[h][:UNIT] + vke[h]], axis=1)
        loc_ref[s, :] = reads[h][:UNIT] + vkr[h]
        st_ref[s, :] = recept[s] * emid[s] + reads[h][UNIT:]


def join_kernel(
    n,
    nh,
    tp_ref,
    loc_ref,
    st_ref,
    r_ref,
    k_ref,
    v_ref,
    g_ref,
    rw_ref,
    gain_ref,
    bias_ref,
    skip_ref,
    w_hbm,
    out_ref,
    slabs,
    sbuf,
    sin,
    mixed,
    wbuf,
    near_out,
    near_in,
    far_out,
    far_in,
    acc,
    send1,
    recv1,
    send2,
    recv2,
    send3,
    recv3,
    send4,
    recv4,
    w_sem,
):
    me = lax.axis_index("seq")
    mh = lax.axis_index("head")
    hi, lo = mh // 2, mh % 2
    far = nh // 2
    channels, length = r_ref.shape
    units = channels // UNIT
    own = max(1, units // n)
    share = channels // n
    rows = out_ref.shape[0]

    w_copy = pltpu.make_async_copy(w_hbm, wbuf, w_sem)
    w_copy.start()

    barrier = pltpu.get_barrier_semaphore()
    for off in range(1, n):
        pl.semaphore_signal(barrier, inc=1, device_id={"seq": (me + off) % n}, device_id_type=MESH)
    for off in range(1, nh):
        pl.semaphore_signal(barrier, inc=1, device_id={"head": (mh + off) % nh}, device_id_type=MESH)
    pl.semaphore_wait(barrier, n - 1 + nh - 1)

    def first_row(d):
        return pl.multiple_of((d * share) // UNIT * UNIT, UNIT)

    sends = []
    for off in range(1, n):
        d = (me + off) % n
        copy = pltpu.make_async_remote_copy(
            src_ref=tp_ref.at[pl.ds(first_row(d), own * UNIT)],
            dst_ref=slabs.at[me],
            send_sem=send1.at[off],
            recv_sem=recv1.at[off],
            device_id={"seq": d},
            device_id_type=MESH,
        )
        copy.start()
        sends.append(copy)
    slabs[me] = tp_ref[pl.ds(first_row(me), own * UNIT), :]
    for copy in sends:
        copy.wait()

    state = [jnp.zeros((UNIT, UNIT), F32) for _ in range(own)]
    for j in range(n):
        for u in range(own):
            sbuf[j, u * UNIT : (u + 1) * UNIT, :] = state[u]
        if j + 1 < n:
            for u in range(own):
                item = slabs[j, u * UNIT : (u + 1) * UNIT, :]
                state[u] = mm(state[u], item[:, :UNIT]) + item[:, UNIT:]

    inner = pl.multiple_of((me * share) % UNIT, min(share, UNIT))
    mine = pl.ds(pl.multiple_of(me * share, share), share)
    sends = []
    for off in range(1, n):
        d = (me + off) % n
        copy = pltpu.make_async_remote_copy(
            src_ref=sbuf.at[d, pl.ds(inner, share)],
            dst_ref=sin.at[mine],
            send_sem=send2.at[off],
            recv_sem=recv2.at[off],
            device_id={"seq": d},
            device_id_type=MESH,
        )
        copy.start()
        sends.append(copy)
    sin[mine, :] = sbuf[me, pl.ds(inner, share), :]

    for copy in sends:
        copy.wait()

    def finish(p, carry):
        base = pl.multiple_of(p * 128, 128)
        rw = columns_of(rw_ref, p, 1)
        gain = columns_of(gain_ref, p, 1)
        bias = columns_of(bias_ref, p, 1)
        for u in range(2):
            s = pl.ds(base + u * UNIT, UNIT)
            c = slice(u * UNIT, (u + 1) * UNIT)
            y = loc_ref[s, :] + mm(sin[s, :], st_ref[s, :])
            y = y - jnp.mean(y, axis=0, keepdims=True)
            q = jnp.mean(y * y, axis=0, keepdims=True)
            normed = y * lax.rsqrt(q + 0.00064) * gain[c] + bias[c]
            rk = r_ref[s, :].astype(F32) * k_ref[s, :].astype(F32) * rw[c]
            bonus = jnp.sum(rk, axis=0, keepdims=True) * v_ref[s, :].astype(F32)
            mixed[s, :] = ((normed + bonus) * g_ref[s, :].astype(F32)).astype(BF16)
        return carry

    lax.fori_loop(0, units // 2, finish, 0)
    w_copy.wait()

    tile = 256

    def block(j, put):
        def body(i, carry):
            at = pl.multiple_of(i * tile, tile)
            wt = wbuf[pl.ds(pl.multiple_of(j * rows, rows) + at, tile), :]
            put(pl.ds(at, tile), jnp.dot(wt, mixed[...], preferred_element_type=F32))
            return carry

        lax.fori_loop(0, rows // tile, body, 0)

    near = []
    for f in range(far):
        h = (hi + 1 + f) % far

        def put(s, x, f=f):
            near_out[f, s, :] = x.astype(BF16)

        block(h * 2 + (1 - lo), put)
        copy = pltpu.make_async_remote_copy(
            src_ref=near_out.at[f],
            dst_ref=near_in.at[f],
            send_sem=send3.at[f],
            recv_sem=recv3.at[f],
            device_id={"head": hi * 2 + (1 - lo)},
            device_id_type=MESH,
        )
        copy.start()
        near.append(copy)
    away = []
    for f in range(far - 1):
        h = (hi + 1 + f) % far

        def put(s, x):
            acc[s, :] = x

        block(h * 2 + lo, put)
        near[f].wait()
        far_out[f] = (acc[...] + near_in[f].astype(F32)).astype(BF16)
        copy = pltpu.make_async_remote_copy(
            src_ref=far_out.at[f],
            dst_ref=far_in.at[f],
            send_sem=send4.at[f],
            recv_sem=recv4.at[f],
            device_id={"head": h * 2 + lo},
            device_id_type=MESH,
        )
        copy.start()
        away.append(copy)

    def put_last(s, x):
        acc[s, :] = x + skip_ref[s, :].astype(F32)

    block(mh, put_last)
    near[far - 1].wait()
    acc[...] += near_in[far - 1].astype(F32)
    for f in range(far - 1):
        away[f].wait()
        acc[...] += far_in[f].astype(F32)
    out_ref[...] = acc[...].astype(BF16)


def on_device(n, nh, skip, r, k, v, g, w, a, erasure, reward, gain, bias, weights):
    channels, length = r.shape
    rows = GROUP * UNIT
    flat = lambda x: x.reshape(channels // 128, 128)
    block = pl.BlockSpec((rows, length), lambda i: (i, 0))
    whole = pl.BlockSpec(memory_space=pltpu.VMEM)
    tp, loc, st = pl.pallas_call(
        local_kernel,
        grid=(channels // rows,),
        in_specs=[block] * 5 + [pl.BlockSpec((channels // 128, 128), lambda i: (0, 0))],
        out_specs=[pl.BlockSpec((rows, 2 * UNIT), lambda i: (i, 0)), block, block],
        out_shape=[
            jax.ShapeDtypeStruct((channels, 2 * UNIT), F32),
            jax.ShapeDtypeStruct((channels, length), F32),
            jax.ShapeDtypeStruct((channels, length), F32),
        ],
        compiler_params=pltpu.CompilerParams(vmem_limit_bytes=24 * 1024 * 1024),
        name="local",
    )(r, k, v, w, a, flat(erasure))
    own = max(1, channels // UNIT // n)
    out_rows = skip.shape[0]
    far = nh // 2
    dma = pltpu.SemaphoreType.DMA
    return pl.pallas_call(
        functools.partial(join_kernel, n, nh),
        out_shape=jax.ShapeDtypeStruct(skip.shape, BF16),
        in_specs=[whole] * 11 + [pl.BlockSpec(memory_space=pl.ANY)],
        out_specs=whole,
        scratch_shapes=[
            pltpu.VMEM((n, own * UNIT, 2 * UNIT), F32),
            pltpu.VMEM((n, own * UNIT, UNIT), F32),
            pltpu.VMEM((channels, UNIT), F32),
            pltpu.VMEM((channels, length), BF16),
            pltpu.VMEM(weights.shape, BF16),
            pltpu.VMEM((far, out_rows, length), BF16),
            pltpu.VMEM((far, out_rows, length), BF16),
            pltpu.VMEM((far, out_rows, length), BF16),
            pltpu.VMEM((far, out_rows, length), BF16),
            pltpu.VMEM((out_rows, length), F32),
            dma((n,)),
            dma((n,)),
            dma((n,)),
            dma((n,)),
            dma((far,)),
            dma((far,)),
            dma((far,)),
            dma((far,)),
            dma,
        ],
        compiler_params=pltpu.CompilerParams(
            collective_id=0, has_side_effects=True, vmem_limit_bytes=40 * 1024 * 1024
        ),
        name="join",
    )(tp, loc, st, r, k, v, g, flat(reward), flat(gain), flat(bias), skip, weights)


def solution(mesh):
    n, nh = mesh.shape["seq"], mesh.shape["head"]
    both, one = P("head", "seq"), P("head")
    return jax.shard_map(
        functools.partial(on_device, n, nh),
        mesh=mesh,
        in_specs=(both,) * 7 + (one,) * 4 + (P(None, "head"),),
        out_specs=both,
        check_vma=False,
    )
```

time: 274 us -> 71.5 us (0.26)
  the two profiles are of different devices: /device:TPU:0 before, /device:TPU:24 now
where the time goes in v1:
time: 71.5 us; the launch traced here: 70.9 us
  Pallas kernels  54.5 us (76%)
  local copies, waits for them, and re-layouts  16.3 us (23%)
    pallas_call x1, Pallas kernels, on_device(): pl.pallas_call(functools.partial(join_kernel, n, nh), out_shape=jax.Shape...  43.5 us
    unnamed x31, local copies, waits for them, and re-layouts  16.3 us
    pallas_call x1, Pallas kernels, on_device(): pl.pallas_call(local_kernel, grid=(channels // rows,), in_specs=[block] *...  11 us

profile of v1, /device:TPU:24, one launch (start us, length us, event | category | flops | bytes accessed | tf_op | source)
XLA Modules:
  0.0 70.9 jit_solution(5358680248570521223)
XLA Ops:
  0.0 0.0 copy-start.1
  0.0 0.9 %copy-done.1 = bf16[1024,128]{1,0:T(8,128)(2,1)S(1)} copy-done((bf16[1024,128]{1,0:T(8,128)(2,1)S(1)}, bf16[1024,128]{1,0:T(8,128)(2,1)}, u32[]{:S(2)}) %copy-start.1) | copy-done | bytes 262168
  1.0 0.0 copy-start.3
  1.0 0.9 %copy-done.3 = bf16[1024,128]{1,0:T(8,128)(2,1)S(1)} copy-done((bf16[1024,128]{1,0:T(8,128)(2,1)S(1)}, bf16[1024,128]{1,0:T(8,128)(2,1)}, u32[]{:S(2)}) %copy-start.3) | copy-done | bytes 262168
  1.9 0.0 copy-start.5
  1.9 0.9 %copy-done.5 = bf16[1024,128]{1,0:T(8,128)(2,1)S(1)} copy-done((bf16[1024,128]{1,0:T(8,128)(2,1)S(1)}, bf16[1024,128]{1,0:T(8,128)(2,1)}, u32[]{:S(2)}) %copy-start.5) | copy-done | bytes 262168
  2.9 0.0 copy-start.7
  2.9 0.9 %copy-done.7 = bf16[1024,128]{1,0:T(8,128)(2,1)S(1)} copy-done((bf16[1024,128]{1,0:T(8,128)(2,1)S(1)}, bf16[1024,128]{1,0:T(8,128)(2,1)}, u32[]{:S(2)}) %copy-start.7) | copy-done | bytes 262168
  3.8 0.0 copy-start.8
  3.8 0.9 %copy-done.8 = bf16[1024,128]{1,0:T(8,128)(2,1)S(1)} copy-done((bf16[1024,128]{1,0:T(8,128)(2,1)S(1)}, bf16[1024,128]{1,0:T(8,128)(2,1)}, u32[]{:S(2)}) %copy-start.8) | copy-done | bytes 262168
  4.8 0.0 copy-start.11
  4.8 0.7 copy-done.11
  5.4 11.0 %local.1 = (f32[1024,128]{1,0:T(8,128)S(1)}, f32[1024,128]{1,0:T(8,128)S(1)}, f32[1024,128]{1,0:T(8,128)S(1)}) custom-call(bf16[1024,128]{1,0:T(8,128)(2,1)S(1)} %copy-done.1, bf16[1024,128]{1,0:T(8,128)(2,1)S(1)} %copy-done.3, bf16[1024,128]{1,0:T(8,128)(2,1)S(1)} %copy-done.5, bf16[1024,128]{1,0:T(8,128)(2,1)S(1)} %copy-done.7, ...), custom_call_target="tpu_custom_call" | custom-call | tf_op jit(solution)/shard_map/local/pallas_call | solution.py:314
  16.4 0.0 copy-start
  16.4 3.4 %copy-done = bf16[4096,1024]{1,0:T(8,128)(2,1)S(1)} copy-done((bf16[4096,1024]{1,0:T(8,128)(2,1)S(1)}, bf16[4096,1024]{1,0:T(8,128)(2,1)}, u32[]{:S(2)}) %copy-start) | copy-done | bytes 8388632
  19.8 0.0 copy-start.2
  19.8 0.9 %copy-done.2 = bf16[1024,128]{1,0:T(8,128)(2,1)S(1)} copy-done((bf16[1024,128]{1,0:T(8,128)(2,1)S(1)}, bf16[1024,128]{1,0:T(8,128)(2,1)}, u32[]{:S(2)}) %copy-start.2) | copy-done | bytes 262168
  20.8 0.0 copy-start.4
  20.8 0.9 %copy-done.4 = bf16[1024,128]{1,0:T(8,128)(2,1)S(1)} copy-done((bf16[1024,128]{1,0:T(8,128)(2,1)S(1)}, bf16[1024,128]{1,0:T(8,128)(2,1)}, u32[]{:S(2)}) %copy-start.4) | copy-done | bytes 262168
  21.7 0.9 %copy-done.6 = bf16[1024,128]{1,0:T(8,128)(2,1)S(1)} copy-done((bf16[1024,128]{1,0:T(8,128)(2,1)S(1)}, bf16[1024,128]{1,0:T(8,128)(2,1)}, u32[]{:S(2)}) %copy-start.6) | copy-done | bytes 262168
  22.7 0.0 copy-start.9
  22.7 0.9 %copy-done.9 = bf16[1024,128]{1,0:T(8,128)(2,1)S(1)} copy-done((bf16[1024,128]{1,0:T(8,128)(2,1)S(1)}, bf16[1024,128]{1,0:T(8,128)(2,1)}, u32[]{:S(2)}) %copy-start.9) | copy-done | bytes 262168
  23.6 0.0 copy-start.10
  23.6 0.9 %copy-done.10 = bf16[1024,128]{1,0:T(8,128)(2,1)S(1)} copy-done((bf16[1024,128]{1,0:T(8,128)(2,1)S(1)}, bf16[1024,128]{1,0:T(8,128)(2,1)}, u32[]{:S(2)}) %copy-start.10) | copy-done | bytes 262168
  24.6 0.0 copy-start.12
  24.6 0.7 copy-done.12
  25.3 0.0 copy-start.13
  25.3 0.7 copy-done.13
  25.9 0.0 copy-start.14
  25.9 0.7 copy-done.14
  26.6 43.5 %join.1 = bf16[1024,128]{1,0:T(8,128)(2,1)S(1)} custom-call(f32[1024,128]{1,0:T(8,128)S(1)} %get-tuple-element.8.tp_ref, f32[1024,128]{1,0:T(8,128)S(1)} %get-tuple-element.9.loc_ref, f32[1024,128]{1,0:T(8,128)S(1)} %get-tuple-element.10.st_ref, bf16[1024,128]{1,0:T(8,128)(2,1)S(1)} %copy-done.2, bf16[1024,128]{1,0:T(8,128)(2,1)S(1)} %copy-done.4, ...), custom_call_target="tpu_custom_call" | custom-call | tf_op jit(solution)/shard_map/join/pallas_call | solution.py:331
  70.2 0.7 copy.14
  (1 shorter events, 0.0 us)
Async XLA Ops:
  0.0 0.9 %copy-start.1 = (bf16[1024,128]{1,0:T(8,128)(2,1)S(1)}, bf16[1024,128]{1,0:T(8,128)(2,1)}, u32[]{:S(2)}) copy-start(bf16[1024,128]{1,0:T(8,128)(2,1)} %r_ref.3) | copy-start | bytes 786436
  1.0 0.9 %copy-start.3 = (bf16[1024,128]{1,0:T(8,128)(2,1)S(1)}, bf16[1024,128]{1,0:T(8,128)(2,1)}, u32[]{:S(2)}) copy-start(bf16[1024,128]{1,0:T(8,128)(2,1)} %k_ref.3) | copy-start | bytes 786436
  1.9 0.9 %copy-start.5 = (bf16[1024,128]{1,0:T(8,128)(2,1)S(1)}, bf16[1024,128]{1,0:T(8,128)(2,1)}, u32[]{:S(2)}) copy-start(bf16[1024,128]{1,0:T(8,128)(2,1)} %v_ref.3) | copy-start | bytes 786436
  2.9 0.9 %copy-start.7 = (bf16[1024,128]{1,0:T(8,128)(2,1)S(1)}, bf16[1024,128]{1,0:T(8,128)(2,1)}, u32[]{:S(2)}) copy-start(bf16[1024,128]{1,0:T(8,128)(2,1)} %w_ref.1) | copy-start | bytes 786436
  3.8 0.9 %copy-start.8 = (bf16[1024,128]{1,0:T(8,128)(2,1)S(1)}, bf16[1024,128]{1,0:T(8,128)(2,1)}, u32[]{:S(2)}) copy-start(bf16[1024,128]{1,0:T(8,128)(2,1)} %a_ref.1) | copy-start | bytes 786436
  4.8 0.7 copy-start.11
  16.4 3.4 %copy-start = (bf16[4096,1024]{1,0:T(8,128)(2,1)S(1)}, bf16[4096,1024]{1,0:T(8,128)(2,1)}, u32[]{:S(2)}) copy-start(bf16[4096,1024]{1,0:T(8,128)(2,1)} %w_hbm.1) | copy-start | bytes 25165828
  19.8 0.9 %copy-start.2 = (bf16[1024,128]{1,0:T(8,128)(2,1)S(1)}, bf16[1024,128]{1,0:T(8,128)(2,1)}, u32[]{:S(2)}) copy-start(bf16[1024,128]{1,0:T(8,128)(2,1)} %r_ref.3) | copy-start | bytes 786436
  20.8 0.9 %copy-start.4 = (bf16[1024,128]{1,0:T(8,128)(2,1)S(1)}, bf16[1024,128]{1,0:T(8,128)(2,1)}, u32[]{:S(2)}) copy-start(bf16[1024,128]{1,0:T(8,128)(2,1)} %k_ref.3) | copy-start | bytes 786436
  21.7 0.9 %copy-start.6 = (bf16[1024,128]{1,0:T(8,128)(2,1)S(1)}, bf16[1024,128]{1,0:T(8,128)(2,1)}, u32[]{:S(2)}) copy-start(bf16[1024,128]{1,0:T(8,128)(2,1)} %v_ref.3) | copy-start | bytes 786436
  22.7 0.9 %copy-start.9 = (bf16[1024,128]{1,0:T(8,128)(2,1)S(1)}, bf16[1024,128]{1,0:T(8,128)(2,1)}, u32[]{:S(2)}) copy-start(bf16[1024,128]{1,0:T(8,128)(2,1)} %g_ref.1) | copy-start | bytes 786436
  23.6 0.9 %copy-start.10 = (bf16[1024,128]{1,0:T(8,128)(2,1)S(1)}, bf16[1024,128]{1,0:T(8,128)(2,1)}, u32[]{:S(2)}) copy-start(bf16[1024,128]{1,0:T(8,128)(2,1)} %skip_ref.1) | copy-start | bytes 786436
  24.6 0.7 copy-start.12
  25.3 0.7 copy-start.13
  25.9 0.7 copy-start.14

commit v2 on v1

v2 whole, which is shorter than its diff:
```python
import functools

import jax
import jax.numpy as jnp
from jax import lax
from jax.experimental import pallas as pl
from jax.experimental.pallas import tpu as pltpu
from jax.sharding import PartitionSpec as P

MESH = pl.DeviceIdType.MESH
UNIT = 64
GROUP = 4
F32 = jnp.float32
BF16 = jnp.bfloat16


def split(x):
    hi = x.astype(BF16)
    return hi, (x - hi.astype(F32)).astype(BF16)


def mm(a, b, ca=1, cb=0, passes=3):
    dims = (((ca,), (cb,)), ((), ()))
    if passes == 1:
        return lax.dot_general(a.astype(BF16), b.astype(BF16), dims, preferred_element_type=F32)
    if a.dtype == BF16:
        bh, bl = split(b)
        a2 = jnp.concatenate([a, a], axis=ca)
        b2 = jnp.concatenate([bh, bl], axis=cb)
        return lax.dot_general(a2, b2, dims, preferred_element_type=F32)
    ah, al = split(a)
    bh, bl = split(b)
    a3 = jnp.concatenate([ah, ah, al], axis=ca)
    b3 = jnp.concatenate([bh, bl, bh], axis=cb)
    return lax.dot_general(a3, b3, dims, preferred_element_type=F32)


def columns_of(row_ref, first, count):
    i = lax.broadcasted_iota(jnp.int32, (128, 128), 0)
    j = lax.broadcasted_iota(jnp.int32, (128, 128), 1)
    eye = i == j
    out = []
    for n in range(count):
        row = row_ref[pl.ds(first + n, 1), :]
        out.append(jnp.sum(jnp.where(eye, jnp.broadcast_to(row, (128, 128)), 0.0), axis=1, keepdims=True))
    return jnp.concatenate(out, axis=0) if count > 1 else out[0]


def local_group(p, r_ref, k_ref, v_ref, w_ref, a_ref, er_ref, tp_ref, loc_ref, st_ref):
    length = r_ref.shape[1]
    first = pl.multiple_of(p * (GROUP * UNIT), GROUP * UNIT)
    rows = pl.ds(first, GROUP * UNIT)
    mid_at = length // 2 - 1
    si = lax.broadcasted_iota(jnp.int32, (length, length), 0)
    ti = lax.broadcasted_iota(jnp.int32, (length, length), 1)
    ones = jnp.where(si <= ti, 1.0, 0.0) - jnp.where(si <= mid_at, 1.0, 0.0)
    w16 = w_ref[rows, :]
    c = jnp.dot(w16, ones.astype(BF16), preferred_element_type=F32)
    w = w16.astype(F32)
    er = columns_of(er_ref, p * (GROUP // 2), GROUP // 2)
    k = k_ref[rows, :].astype(F32)
    scaled = k * er
    heads = range(GROUP)
    sl = [slice(h * UNIT, (h + 1) * UNIT) for h in heads]
    kk = jnp.concatenate(
        [scaled[s] * lax.rsqrt(jnp.sum(scaled[s] * scaled[s], axis=0, keepdims=True) + 1e-06) for s in sl], axis=0
    )
    back = jnp.exp(-c)
    pulled_back = a_ref[rows, :].astype(F32) * kk * back
    keys_back = k * back
    removal = -kk * jnp.exp(c - w)
    recept = r_ref[rows, :].astype(F32) * jnp.exp(c)
    emid = jnp.exp(w[:, 0:1] - c[:, 0:1])
    eend = jnp.exp(c[:, length - 1 :])
    etot = emid * eend
    pulled_end = pulled_back * eend
    keys_end = keys_back * eend

    before = si < ti
    upto = si <= ti
    mix = [
        mm(
            jnp.concatenate([pulled_back[s], keys_back[s]], axis=1),
            jnp.concatenate([removal[s], recept[s]], axis=1),
            0,
            0,
        )
        for s in sl
    ]
    pair_mix = [jnp.where(before, m[:length, :length], 0.0) for m in mix]
    key_mix = [jnp.where(before, m[length:, :length], 0.0) for m in mix]
    pair_read = [jnp.where(upto, m[:length, length:], 0.0) for m in mix]
    key_read = [jnp.where(upto, m[length:, length:], 0.0) for m in mix]
    eye = jnp.where(si == ti, 1.0, 0.0)
    size = 1
    inv = None
    while size < length:
        joins = (si // (2 * size) == ti // (2 * size)) & (si // size != ti // size)
        off = [jnp.where(joins, m, 0.0) for m in pair_mix]
        if inv is None:
            inv = [eye + o for o in off]
        else:
            half = [mm(n, o) for n, o in zip(inv, off)]
            inv = [n + mm(x, n) for n, x in zip(inv, half)]
        size *= 2
    v16 = v_ref[rows, :]
    vk = [mm(v16[s], m) for s, m in zip(sl, key_mix)]
    solved = [mm(jnp.concatenate([x, removal[s]], axis=0), n) for x, s, n in zip(vk, sl, inv)]
    solved = [jnp.concatenate([x[:UNIT], x[UNIT:] * emid[s]], axis=0) for x, s in zip(solved, sl)]
    ends = [mm(x, pulled_end[s], 1, 1) for x, s in zip(solved, sl)]
    vke = [mm(v16[s], keys_end[s], 1, 1) for s in sl]
    reads = [mm(x, p) for x, p in zip(solved, pair_read)]
    vkr = [mm(v16[s], m) for s, m in zip(sl, key_read)]
    diag = lax.broadcasted_iota(jnp.int32, (UNIT, UNIT), 0) == lax.broadcasted_iota(jnp.int32, (UNIT, UNIT), 1)
    for h in heads:
        s = sl[h]
        d = pl.ds(first + h * UNIT, UNIT)
        trans = ends[h][UNIT:] + jnp.where(diag, jnp.broadcast_to(etot[s], (UNIT, UNIT)), 0.0)
        tp_ref[d, :] = jnp.concatenate([trans, ends[h][:UNIT] + vke[h]], axis=1)
        loc_ref[d, :] = reads[h][:UNIT] + vkr[h]
        st_ref[d, :] = recept[s] * emid[s] + reads[h][UNIT:]


def kernel(n, nh, *refs):
    names = INPUTS + ("out",) + SCRATCH
    join(n, nh, dict(zip(names, refs)))


INPUTS = ("r", "k", "v", "w", "a", "g", "er", "rw", "gain", "bias", "skip", "weights")
SCRATCH = tuple(x + "_v" for x in INPUTS) + (
    "tp", "loc", "st", "bonus", "slabs", "sbuf", "sin", "mixed",
    "near_out", "near_in", "far_out", "far_in", "acc",
    "send1", "recv1", "send2", "recv2", "send3", "recv3", "send4", "recv4", "load",
)
CHUNKS = 4


def join(n, nh, ref):
    me = lax.axis_index("seq")
    mh = lax.axis_index("head")
    hi, lo = mh // 2, mh % 2
    far = nh // 2
    here = {x: ref[x + "_v"] for x in INPUTS}
    channels, length = here["r"].shape
    units = channels // UNIT
    own = max(1, units // n)
    share = channels // n
    part = min(share, UNIT)
    rows = ref["out"].shape[0]
    slabs, sbuf, sin, mixed, acc = (ref[x] for x in ("slabs", "sbuf", "sin", "mixed", "acc"))
    tp, loc, st, bonus = (ref[x] for x in ("tp", "loc", "st", "bonus"))

    order = ("er", "k", "w", "a", "r", "v", "rw", "gain", "bias", "g", "skip", "weights")
    loads = {}
    for i, x in enumerate(order):
        loads[x] = pltpu.make_async_copy(ref[x], here[x], ref["load"].at[i])
        loads[x].start()

    barrier = pltpu.get_barrier_semaphore()
    for off in range(1, n):
        pl.semaphore_signal(barrier, inc=1, device_id={"seq": (me + off) % n}, device_id_type=MESH)
    for off in range(1, nh):
        pl.semaphore_signal(barrier, inc=1, device_id={"head": (mh + off) % nh}, device_id_type=MESH)
    for x in order[:6]:
        loads[x].wait()
    pl.semaphore_wait(barrier, n - 1 + nh - 1)

    def state_copy(d):
        off = (d - me + n) % n
        row = pl.multiple_of((d * share) // UNIT * UNIT, UNIT)
        return pltpu.make_async_remote_copy(
            src_ref=tp.at[pl.ds(row, own * UNIT)],
            dst_ref=slabs.at[me],
            send_sem=ref["send1"].at[off],
            recv_sem=ref["recv1"].at[off],
            device_id={"seq": d},
            device_id_type=MESH,
        )

    groups = units // GROUP
    owners = GROUP * UNIT // share

    def local_step(i, carry):
        p = (me // owners + 1 + i) % groups
        local_group(p, *(here[x] for x in ("r", "k", "v", "w", "a", "er")), tp, loc, st)
        for q in range(owners):
            d = p * owners + q

            @pl.when(d != me)
            def _():
                state_copy(d).start()

        return carry

    lax.fori_loop(0, groups, local_step, 0)
    slabs[me] = tp[pl.ds(pl.multiple_of((me * share) // UNIT * UNIT, UNIT), own * UNIT), :]

    for x in order[6:11]:
        loads[x].wait()

    def bonus_step(p, carry):
        base = pl.multiple_of(p * 128, 128)
        rw = columns_of(here["rw"], p, 1)
        for u in range(2):
            s = pl.ds(base + u * UNIT, UNIT)
            rk = here["r"][s, :].astype(F32) * here["k"][s, :].astype(F32) * rw[u * UNIT : (u + 1) * UNIT]
            bonus[s, :] = jnp.sum(rk, axis=0, keepdims=True) * here["v"][s, :].astype(F32)
        return carry

    lax.fori_loop(0, units // 2, bonus_step, 0)
    for off in range(1, n):
        state_copy((me + off) % n).wait()

    state = [jnp.zeros((UNIT, UNIT), F32) for _ in range(own)]
    for j in range(n):
        sbuf[j] = jnp.concatenate(state, axis=1).astype(sbuf.dtype)
        if j + 1 < n:
            for u in range(own):
                item = slabs[j, u * UNIT : (u + 1) * UNIT, :]
                state[u] = mm(state[u], item[:, :UNIT]) + item[:, UNIT:]

    inner = pl.multiple_of((me * share) % UNIT, part)
    mine = pl.ds(pl.multiple_of(me * part, part), part)
    sends = []
    for off in range(1, n):
        d = (me + off) % n
        copy = pltpu.make_async_remote_copy(
            src_ref=sbuf.at[d, pl.ds(inner, part)],
            dst_ref=sin.at[mine],
            send_sem=ref["send2"].at[off],
            recv_sem=ref["recv2"].at[off],
            device_id={"seq": d},
            device_id_type=MESH,
        )
        copy.start()
        sends.append(copy)
    sin[mine, :] = sbuf[me, pl.ds(inner, part), :]
    for copy in sends:
        copy.wait()

    def finish(p, carry):
        base = pl.multiple_of(p * 128, 128)
        gain = columns_of(here["gain"], p, 1)
        bias = columns_of(here["bias"], p, 1)
        for u in range(2):
            s = pl.ds(base + u * UNIT, UNIT)
            c = slice(u * UNIT, (u + 1) * UNIT)
            if own == 1:
                arriving = sin[s, :]
            else:
                arriving = sin[pl.ds(pl.multiple_of(p * 2 // own * UNIT, UNIT), UNIT), u % own * UNIT : (u % own + 1) * UNIT]
            y = loc[s, :] + mm(arriving, st[s, :])
            y = y - jnp.mean(y, axis=0, keepdims=True)
            q = jnp.mean(y * y, axis=0, keepdims=True)
            normed = y * lax.rsqrt(q + 0.00064) * gain[c] + bias[c]
            mixed[s, :] = ((normed + bonus[s, :]) * here["g"][s, :].astype(F32)).astype(BF16)
        return carry

    lax.fori_loop(0, units // 2, finish, 0)
    loads["weights"].wait()

    tile = rows // CHUNKS

    def piece(j, c):
        at = pl.multiple_of(j * rows, rows) + c * tile
        return jnp.dot(here["weights"][pl.ds(at, tile), :], mixed[...], preferred_element_type=F32)

    def near_copy(f, c):
        s = pl.ds(c * tile, tile)
        return pltpu.make_async_remote_copy(
            src_ref=ref["near_out"].at[f, s],
            dst_ref=ref["near_in"].at[f, s],
            send_sem=ref["send3"].at[f, c],
            recv_sem=ref["recv3"].at[f, c],
            device_id={"head": hi * 2 + (1 - lo)},
            device_id_type=MESH,
        )

    def far_copy(f, c):
        s = pl.ds(c * tile, tile)
        return pltpu.make_async_remote_copy(
            src_ref=ref["far_out"].at[f, s],
            dst_ref=ref["far_in"].at[f, s],
            send_sem=ref["send4"].at[f, c],
            recv_sem=ref["recv4"].at[f, c],
            device_id={"head": (hi + 1 + f) % far * 2 + lo},
            device_id_type=MESH,
        )

    def near_all(f):
        for c in range(CHUNKS):
            h = (hi + 1 + f) % far
            ref["near_out"][f, c * tile : (c + 1) * tile, :] = piece(h * 2 + (1 - lo), c).astype(BF16)
            near_copy(f, c).start()

    near_all(0)
    for f in range(far - 1):
        for c in range(CHUNKS):
            s = slice(c * tile, (c + 1) * tile)
            x = piece((hi + 1 + f) % far * 2 + lo, c)
            near_copy(f, c).wait()
            ref["far_out"][f, s, :] = (x + ref["near_in"][f, s, :].astype(F32)).astype(BF16)
            far_copy(f, c).start()
        near_all(f + 1)
    for c in range(CHUNKS):
        s = slice(c * tile, (c + 1) * tile)
        x = piece(mh, c) + here["skip"][s, :].astype(F32)
        near_copy(far - 1, c).wait()
        acc[s, :] = x + ref["near_in"][far - 1, s, :].astype(F32)
    for c in range(CHUNKS):
        s = slice(c * tile, (c + 1) * tile)
        x = acc[s, :]
        for f in range(far - 1):
            far_copy(f, c).wait()
            x = x + ref["far_in"][f, s, :].astype(F32)
        ref["out"][s, :] = x.astype(BF16)


def on_device(n, nh, skip, r, k, v, g, w, a, erasure, reward, gain, bias, weights):
    channels, length = r.shape
    flat = lambda x: x.reshape(channels // 128, 128)
    own = max(1, channels // UNIT // n)
    part = min(channels // n, UNIT)
    rows = skip.shape[0]
    far = nh // 2
    dma = pltpu.SemaphoreType.DMA
    operands = (r, k, v, w, a, g, flat(erasure), flat(reward), flat(gain), flat(bias), skip, weights)
    return pl.pallas_call(
        functools.partial(kernel, n, nh),
        out_shape=jax.ShapeDtypeStruct(skip.shape, BF16),
        in_specs=[pl.BlockSpec(memory_space=pl.ANY)] * len(operands),
        out_specs=pl.BlockSpec(memory_space=pltpu.VMEM),
        scratch_shapes=[pltpu.VMEM(x.shape, x.dtype) for x in operands]
        + [
            pltpu.VMEM((channels, 2 * UNIT), F32),
            pltpu.VMEM((channels, length), F32),
            pltpu.VMEM((channels, length), F32),
            pltpu.VMEM((channels, length), F32),
            pltpu.VMEM((n, own * UNIT, 2 * UNIT), F32),
            pltpu.VMEM((n, UNIT, own * UNIT), F32),
            pltpu.VMEM((n * part, own * UNIT), F32),
            pltpu.VMEM((channels, length), BF16),
            pltpu.VMEM((far, rows, length), BF16),
            pltpu.VMEM((far, rows, length), BF16),
            pltpu.VMEM((far, rows, length), BF16),
            pltpu.VMEM((far, rows, length), BF16),
            pltpu.VMEM((rows, length), F32),
            dma((n,)),
            dma((n,)),
            dma((n,)),
            dma((n,)),
            dma((far, CHUNKS)),
            dma((far, CHUNKS)),
            dma((far, CHUNKS)),
            dma((far, CHUNKS)),
            dma((len(operands),)),
        ],
        compiler_params=pltpu.CompilerParams(
            collective_id=0, has_side_effects=True, vmem_limit_bytes=62 * 1024 * 1024
        ),
        name="timemix",
    )(*operands)


def solution(mesh):
    n, nh = mesh.shape["seq"], mesh.shape["head"]
    both, one = P("head", "seq"), P("head")
    return jax.shard_map(
        functools.partial(on_device, n, nh),
        mesh=mesh,
        in_specs=(both,) * 7 + (one,) * 4 + (P(None, "head"),),
        out_specs=both,
        check_vma=False,
    )
```

time: 71.5 us -> 42.8 us (0.60)
  the two profiles are of different devices: /device:TPU:24 before, /device:TPU:0 now
where the time goes in v2:
time: 42.8 us; the launch traced here: 42.7 us
  Pallas kernels  41 us (96%)
  local copies, waits for them, and re-layouts  1.67 us (4%)
    pallas_call x1, Pallas kernels, on_device(): pl.pallas_call(functools.partial(kernel, n, nh), out_shape=jax.ShapeDtype...  41 us
    unnamed x1, local copies, waits for them, and re-layouts  1.67 us

profile of v2, /device:TPU:0, one launch (start us, length us, event | category | flops | bytes accessed | tf_op | source)
XLA Modules:
  0.0 42.7 jit_solution(14463938154540550746)
XLA Ops:
  0.0 41.0 %timemix.1 = bf16[1024,128]{1,0:T(8,128)(2,1)} custom-call(bf16[1024,128]{1,0:T(8,128)(2,1)} %refs_0_.1, bf16[1024,128]{1,0:T(8,128)(2,1)} %refs_1_.1, bf16[1024,128]{1,0:T(8,128)(2,1)} %refs_2_.1, bf16[1024,128]{1,0:T(8,128)(2,1)} %refs_3_.1, bf16[1024,128]{1,0:T(8,128)(2,1)} %refs_4_.1, bf16[1024,128]{1,0:T(8,128)(2,1)} %refs_5_.1, f32[8,128]{1,0:T(8,128)} %bitcast.4, ...), custom_call_target="tpu_custom_call" | custom-call | tf_op jit(solution)/shard_map/timemix/pallas_call | solution.py:328
  41.0 1.7 %copy.14 = bf16[1024,128]{1,0:T(8,128)(2,1)} copy(bf16[1024,128]{1,0:T(8,128)(2,1)} %timemix.1) | data formatting | bytes 524288

commit v3 on v2

--- a/solution.py
+++ b/solution.py
@@ -100,8 +100,8 @@
         if inv is None:
             inv = [eye + o for o in off]
         else:
-            half = [mm(n, o) for n, o in zip(inv, off)]
-            inv = [n + mm(x, n) for n, x in zip(inv, half)]
+            half = [mm(n, o, passes=1) for n, o in zip(inv, off)]
+            inv = [n + mm(x, n, passes=1) for n, x in zip(inv, half)]
         size *= 2
     v16 = v_ref[rows, :]
     vk = [mm(v16[s], m) for s, m in zip(sl, key_mix)]
@@ -116,7 +116,7 @@
         s = sl[h]
         d = pl.ds(first + h * UNIT, UNIT)
         trans = ends[h][UNIT:] + jnp.where(diag, jnp.broadcast_to(etot[s], (UNIT, UNIT)), 0.0)
-        tp_ref[d, :] = jnp.concatenate([trans, ends[h][:UNIT] + vke[h]], axis=1)
+        tp_ref[d, :] = jnp.concatenate([trans, ends[h][:UNIT] + vke[h]], axis=1).astype(BF16)
         loc_ref[d, :] = reads[h][:UNIT] + vkr[h]
         st_ref[d, :] = recept[s] * emid[s] + reads[h][UNIT:]
 
@@ -163,7 +163,6 @@
         pl.semaphore_signal(barrier, inc=1, device_id={"head": (mh + off) % nh}, device_id_type=MESH)
     for x in order[:6]:
         loads[x].wait()
-    pl.semaphore_wait(barrier, n - 1 + nh - 1)
 
     def state_copy(d):
         off = (d - me + n) % n
@@ -183,6 +182,8 @@
     def local_step(i, carry):
         p = (me // owners + 1 + i) % groups
         local_group(p, *(here[x] for x in ("r", "k", "v", "w", "a", "er")), tp, loc, st)
+        if carry is None:
+            pl.semaphore_wait(barrier, n - 1 + nh - 1)
         for q in range(owners):
             d = p * owners + q
 
@@ -192,7 +193,8 @@
 
         return carry
 
-    lax.fori_loop(0, groups, local_step, 0)
+    local_step(0, None)
+    lax.fori_loop(1, groups, local_step, 0)
     slabs[me] = tp[pl.ds(pl.multiple_of((me * share) // UNIT * UNIT, UNIT), own * UNIT), :]
 
     for x in order[6:11]:
@@ -216,7 +218,7 @@
         sbuf[j] = jnp.concatenate(state, axis=1).astype(sbuf.dtype)
         if j + 1 < n:
             for u in range(own):
-                item = slabs[j, u * UNIT : (u + 1) * UNIT, :]
+                item = slabs[j, u * UNIT : (u + 1) * UNIT, :].astype(F32)
                 state[u] = mm(state[u], item[:, :UNIT]) + item[:, UNIT:]
 
     inner = pl.multiple_of((me * share) % UNIT, part)
@@ -332,13 +334,13 @@
         out_specs=pl.BlockSpec(memory_space=pltpu.VMEM),
         scratch_shapes=[pltpu.VMEM(x.shape, x.dtype) for x in operands]
         + [
-            pltpu.VMEM((channels, 2 * UNIT), F32),
+            pltpu.VMEM((channels, 2 * UNIT), BF16),
             pltpu.VMEM((channels, length), F32),
             pltpu.VMEM((channels, length), F32),
             pltpu.VMEM((channels, length), F32),
-            pltpu.VMEM((n, own * UNIT, 2 * UNIT), F32),
-            pltpu.VMEM((n, UNIT, own * UNIT), F32),
-            pltpu.VMEM((n * part, own * UNIT), F32),
+            pltpu.VMEM((n, own * UNIT, 2 * UNIT), BF16),
+            pltpu.VMEM((n, UNIT, own * UNIT), BF16),
+            pltpu.VMEM((n * part, own * UNIT), BF16),
             pltpu.VMEM((channels, length), BF16),
             pltpu.VMEM((far, rows, length), BF16),
             pltpu.VMEM((far, rows, length), BF16),

time: 42.8 us -> 37.9 us (0.89)
  Pallas kernels: 41 us -> 36 us
    pallas_call x1, Pallas kernels: 41 us -> 36 us  [on_device(): pl.pallas_call(functools.partial(kernel, n, nh), out_shape=jax.ShapeDtype...]
where the time goes in v3:
time: 37.9 us; the launch traced here: 37.7 us
  Pallas kernels  36 us (95%)
  local copies, waits for them, and re-layouts  1.67 us (4%)
    pallas_call x1, Pallas kernels, on_device(): pl.pallas_call(functools.partial(kernel, n, nh), out_shape=jax.ShapeDtype...  36 us
    unnamed x1, local copies, waits for them, and re-layouts  1.67 us

profile of v3, /device:TPU:0, one launch (start us, length us, event | category | flops | bytes accessed | tf_op | source)
XLA Modules:
  0.0 37.7 jit_solution(4969628581779255086)
XLA Ops:
  0.0 36.0 %timemix.1 = bf16[1024,128]{1,0:T(8,128)(2,1)} custom-call(bf16[1024,128]{1,0:T(8,128)(2,1)} %refs_0_.1, bf16[1024,128]{1,0:T(8,128)(2,1)} %refs_1_.1, bf16[1024,128]{1,0:T(8,128)(2,1)} %refs_2_.1, bf16[1024,128]{1,0:T(8,128)(2,1)} %refs_3_.1, bf16[1024,128]{1,0:T(8,128)(2,1)} %refs_4_.1, bf16[1024,128]{1,0:T(8,128)(2,1)} %refs_5_.1, f32[8,128]{1,0:T(8,128)} %bitcast.4, ...), custom_call_target="tpu_custom_call" | custom-call | tf_op jit(solution)/shard_map/timemix/pallas_call | solution.py:330
  36.1 1.7 %copy.14 = bf16[1024,128]{1,0:T(8,128)(2,1)} copy(bf16[1024,128]{1,0:T(8,128)(2,1)} %timemix.1) | data formatting | bytes 524288
